TPU v7x, 32 devices: a whole 2x2x4 slice. The times are simulated.
32 devices in a mesh: dp: 16 (over z, x, core), mp: 2 (over y).
Axes of the slice: x: 2, y: 2, z: 4, core: 2. Of those that a mesh axis runs over, the one named last changes fastest.
Arguments:
- tokens: bfloat16 [64, 256, 1152], P('dp'), may hold values from -6 to 6
- conditioning: bfloat16 [64, 1152], P('dp'), may hold values from -6 to 6
- bucket_ids: int32 [64], P('dp'), may hold values from 0 to 2, as said below
- keep_order: int32 [64, 128], P('dp'), may hold values from 0 to 255, as said below
- group_counts: int32 [16], P('dp'), may hold values from 1 to 4, as said below
- cotangent: bfloat16 [64, 256, 1152], P('dp'), may hold values from -6 to 6
- modulation_weight: bfloat16 [1152, 6912], P('dp'), may hold values from -0.1875 to 0.1875
- modulation_bias: bfloat16 [6912], replicated, may hold values from -3 to 3
- input_weight: bfloat16 [3, 1152, 1152], P(None, 'dp', 'mp'), may hold values from -0.1875 to 0.1875
- query_value_bias: bfloat16 [2, 1152], P(None, 'mp'), may hold values from -3 to 3
- output_weight: bfloat16 [1152, 1152], P('mp', 'dp'), may hold values from -0.75 to 0.75
- output_bias: bfloat16 [1152], replicated, may hold values from -2 to 2
- expand_weight: bfloat16 [1152, 4608], P('dp', 'mp'), may hold values from -0.1875 to 0.1875
- expand_bias: bfloat16 [4608], P('mp'), may hold values from -3 to 3
- shrink_weight: bfloat16 [4608, 1152], P('mp', 'dp'), may hold values from -0.09375 to 0.09375
- shrink_bias: bfloat16 [1152], replicated, may hold values from -2 to 2
Outputs:
- block_out: bfloat16 [64, 256, 1152], P('dp')
- tokens_grad: bfloat16 [64, 256, 1152], P('dp')
- modulation_weight_grad: float32 [1152, 6912], P('dp')
- modulation_bias_grad: float32 [6912], replicated
- input_weight_grad: float32 [3, 1152, 1152], P(None, 'dp', 'mp')
- query_value_bias_grad: float32 [2, 1152], P(None, 'mp')
- output_weight_grad: float32 [1152, 1152], P('mp', 'dp')
- output_bias_grad: float32 [1152], replicated
- expand_weight_grad: float32 [1152, 4608], P('dp', 'mp')
- expand_bias_grad: float32 [4608], P('mp')
- shrink_weight_grad: float32 [4608, 1152], P('mp', 'dp')
- shrink_bias_grad: float32 [1152], replicated
Inputs may be any that keep to these rules, and one draw needn't show every extreme that they name: `bucket_ids`: buckets 0, 1 and 2 stand for grids of 16 x 16, 12 x 20 and 20 x 12 patches. `keep_order`: row i holds 128 distinct slot numbers; its first valid-length entries (half of image i's length) are real token slots of that image chosen at random, the remaining entries are other slots of that image. Group g holds live images in its first group_counts[g] of 4 image slots; in every draw some group is full.
All inputs are finite; a program needn't handle non-finite values.
Results may differ from a plain program's by a relative error of at most 0.015.
The roundings to bfloat16 on the way count: a program that leaves them out, or rounds other values in their place, can miss the bound.
Values may be sent and summed in bfloat16 or wider, within the bound.
A program may use at most 144 MiB of HBM per device.

v0:
```python
import jax
import jax.numpy as jnp
from jax import lax
from jax.sharding import PartitionSpec as P

HEAD_DIM = 72
MICRO = 2
EPSILON = 1e-06


def normalize(rows):
    center = rows - jnp.mean(rows, axis=-1, keepdims=True)
    spread = jnp.mean(center * center, axis=-1, keepdims=True)
    return center * lax.rsqrt(spread + EPSILON)


def modulated(rows, shift, scale):
    return normalize(rows) * (1.0 + scale) + shift


def gelu_tanh(values):
    return jax.nn.gelu(values, approximate=True)


def model_total_sum(partial_value):
    share = lax.psum_scatter(partial_value, "mp", scatter_dimension=2, tiled=True)
    return lax.all_gather(share, "mp", axis=2, tiled=True)


def gather_weights(modulation_weight, input_weight, output_weight, expand_weight, shrink_weight):
    return (
        lax.all_gather(modulation_weight, "dp", axis=0, tiled=True),
        lax.all_gather(input_weight, "dp", axis=1, tiled=True),
        lax.all_gather(output_weight, "dp", axis=1, tiled=True),
        lax.all_gather(expand_weight, "dp", axis=0, tiled=True),
        lax.all_gather(shrink_weight, "dp", axis=1, tiled=True),
    )


def scatter_every(terms):
    return (
        lax.psum_scatter(terms[0], "dp", scatter_dimension=0, tiled=True),
        lax.psum_scatter(terms[1], "dp", scatter_dimension=1, tiled=True),
        lax.psum_scatter(terms[2], "dp", scatter_dimension=1, tiled=True),
        lax.psum_scatter(terms[3], "dp", scatter_dimension=0, tiled=True),
        lax.psum_scatter(terms[4], "dp", scatter_dimension=1, tiled=True),
    )


def attention_scores(query, key_rows, keymask, scale_factor):
    scores = (
        jnp.einsum("bqhd,bkhd->bhqk", query, key_rows, preferred_element_type=jnp.float32)
        * scale_factor
    )
    return jnp.where(keymask[:, None, None, :], scores, -1e30)


def run_micro(tokens_mb, cond_mb, order_mb, valid_mb, grad_mb, full, biases):
    mod_w, incoming_weight, outgoing_weight, expert_weight_rows, narrowing_weight = full
    mod_bias, qv_bias, outgoing_bias, expert_bias_rows, narrowing_bias = biases
    batch, keep = order_mb.shape
    width = tokens_mb.shape[2]
    inner = incoming_weight.shape[2]
    heads_here = inner // HEAD_DIM
    scale_factor = HEAD_DIM ** (-0.5)
    single_float32 = jnp.float32
    bf16 = jnp.bfloat16
    batch_rows = jnp.arange(batch)[:, None]
    keymask = jnp.arange(keep)[None, :] < valid_mb[:, None]
    rowmask = keymask[:, :, None]
    hidden_in = jnp.take_along_axis(tokens_mb, order_mb[:, :, None], axis=1).astype(single_float32)
    silu_cond = jax.nn.silu(cond_mb.astype(single_float32)).astype(bf16)
    modulation = jnp.dot(silu_cond, mod_w, preferred_element_type=single_float32) + mod_bias
    pieces = modulation.reshape(batch, 6, 1, width)
    shift_one, scale_one, gate_one = (pieces[:, 0], pieces[:, 1], pieces[:, 2])
    shift_two, scale_two, gate_two = (pieces[:, 3], pieces[:, 4], pieces[:, 5])
    first, pull_first = jax.vjp(modulated, hidden_in, shift_one, scale_one)
    first_reduced = first.astype(bf16)
    projected_rows = jnp.einsum(
        "mzu,lug->lmzg", first_reduced, incoming_weight, preferred_element_type=single_float32
    )
    query = (projected_rows[0] + qv_bias[0]).astype(bf16).reshape(batch, keep, heads_here, HEAD_DIM)
    key_rows = projected_rows[1].astype(bf16).reshape(batch, keep, heads_here, HEAD_DIM)
    value = (projected_rows[2] + qv_bias[1]).astype(bf16).reshape(batch, keep, heads_here, HEAD_DIM)
    scores = attention_scores(query, key_rows, keymask, scale_factor)
    top = jnp.max(scores, axis=-1, keepdims=True)
    expo = jnp.exp(scores - top)
    total = jnp.sum(expo, axis=-1, keepdims=True)
    probs = expo / total
    log_total = top + jnp.log(total)
    attention_result = (
        jnp.einsum(
            "bhqk,bkhd->bqhd", probs.astype(bf16), value, preferred_element_type=single_float32
        )
        .astype(bf16)
        .reshape(batch, keep, inner)
    )
    attn_out = (
        model_total_sum(
            jnp.einsum(
                "hfc,cj->hfj",
                attention_result,
                outgoing_weight,
                preferred_element_type=single_float32,
            )
        )
        + outgoing_bias
    )
    middle = hidden_in + gate_one * attn_out
    second, pull_second = jax.vjp(modulated, middle, shift_two, scale_two)
    second_reduced = second.astype(bf16)
    preactivation_rows = (
        jnp.einsum(
            "get,tm->gem", second_reduced, expert_weight_rows, preferred_element_type=single_float32
        )
        + expert_bias_rows
    )
    activated, pull_act = jax.vjp(gelu_tanh, preactivation_rows)
    activation_reduced = activated.astype(bf16)
    mlp_out = (
        model_total_sum(
            jnp.einsum(
                "xwl,lc->xwc",
                activation_reduced,
                narrowing_weight,
                preferred_element_type=single_float32,
            )
        )
        + narrowing_bias
    )
    routed_out = jnp.where(rowmask, middle + gate_two * mlp_out, hidden_in)
    block_mb = tokens_mb.at[batch_rows, order_mb].set(routed_out.astype(bf16))
    grad_rows = jnp.take_along_axis(grad_mb, order_mb[:, :, None], axis=1).astype(single_float32)
    grad_final = jnp.where(rowmask, grad_rows, 0.0)
    grad_skip = grad_rows - grad_final
    grad_gate_two = jnp.sum(mlp_out * grad_final, axis=1, keepdims=True)
    grad_mlp = gate_two * grad_final
    perceptron_gradient_reduced = grad_mlp.astype(bf16)
    narrowing_term = jnp.einsum(
        "ehm,eht->mt",
        activation_reduced,
        perceptron_gradient_reduced,
        preferred_element_type=single_float32,
    )
    (grad_pre,) = pull_act(
        jnp.einsum(
            "awm,hm->awh",
            perceptron_gradient_reduced,
            narrowing_weight,
            preferred_element_type=single_float32,
        )
    )
    preactivation_gradient_reduced = grad_pre.astype(bf16)
    widening_term = jnp.einsum(
        "cnq,cne->qe",
        second_reduced,
        preactivation_gradient_reduced,
        preferred_element_type=single_float32,
    )
    grad_second = model_total_sum(
        jnp.einsum(
            "pem,sm->pes",
            preactivation_gradient_reduced,
            expert_weight_rows,
            preferred_element_type=single_float32,
        )
    )
    grad_middle, grad_shift_two, grad_scale_two = pull_second(grad_second)
    grad_middle = grad_middle + grad_final
    grad_gate_one = jnp.sum(attn_out * grad_middle, axis=1, keepdims=True)
    grad_attn = gate_one * grad_middle
    attention_gradient_reduced = grad_attn.astype(bf16)
    output_summand = jnp.einsum(
        "tyo,tyq->oq",
        attention_result,
        attention_gradient_reduced,
        preferred_element_type=single_float32,
    )
    grad_attended = (
        jnp.einsum(
            "znx,ox->zno",
            attention_gradient_reduced,
            outgoing_weight,
            preferred_element_type=single_float32,
        )
        .astype(bf16)
        .reshape(batch, keep, heads_here, HEAD_DIM)
    )
    again = attention_scores(query, key_rows, keymask, scale_factor)
    probs_again = jnp.exp(again - log_total)
    grad_probs = jnp.einsum(
        "bqhd,bkhd->bhqk", grad_attended, value, preferred_element_type=single_float32
    )
    grad_value = jnp.einsum(
        "bhqk,bqhd->bkhd",
        probs_again.astype(bf16),
        grad_attended,
        preferred_element_type=single_float32,
    )
    inner_sum = jnp.sum(probs_again * grad_probs, axis=-1, keepdims=True)
    grad_scores = (probs_again * (grad_probs - inner_sum)).astype(bf16)
    grad_query = (
        jnp.einsum("bhqk,bkhd->bqhd", grad_scores, key_rows, preferred_element_type=single_float32)
        * scale_factor
    )
    grad_key = (
        jnp.einsum("bhqk,bqhd->bkhd", grad_scores, query, preferred_element_type=single_float32)
        * scale_factor
    )
    grad_proj = jnp.stack([grad_query, grad_key, grad_value]).reshape(3, batch, keep, inner)
    query_value_term = jnp.sum(grad_proj[::2], axis=(1, 2))
    projection_gradient_reduced = grad_proj.astype(bf16)
    input_summand = jnp.einsum(
        "iyj,fiyu->fju",
        first_reduced,
        projection_gradient_reduced,
        preferred_element_type=single_float32,
    )
    grad_first = model_total_sum(
        jnp.einsum(
            "pniu,psu->nis",
            projection_gradient_reduced,
            incoming_weight,
            preferred_element_type=single_float32,
        )
    )
    grad_hidden, grad_shift_one, grad_scale_one = pull_first(grad_first)
    grad_total = grad_hidden + grad_middle + grad_skip
    tokens_mb_grad = grad_mb.at[batch_rows, order_mb].set(grad_total.astype(bf16))
    grad_mod = jnp.concatenate(
        [
            grad_shift_one,
            grad_scale_one,
            grad_gate_one,
            grad_shift_two,
            grad_scale_two,
            grad_gate_two,
        ],
        axis=1,
    ).reshape(batch, 6 * width)
    terms = (input_summand, output_summand, widening_term, narrowing_term)
    bias_terms = (
        jnp.sum(grad_mod, axis=0),
        query_value_term,
        jnp.sum(grad_attn, axis=(0, 1)),
        jnp.sum(grad_pre, axis=(0, 1)),
        jnp.sum(grad_mlp, axis=(0, 1)),
    )
    return (block_mb, tokens_mb_grad, terms, bias_terms, silu_cond, grad_mod.astype(bf16))


def body(
    tokens,
    conditioning,
    bucket_ids,
    keep_order,
    group_counts,
    cotangent,
    modulation_weight,
    modulation_bias,
    input_weight,
    query_value_bias,
    output_weight,
    output_bias,
    expand_weight,
    expand_bias,
    shrink_weight,
    shrink_bias,
):
    local = tokens.shape[0]
    per_micro = local // MICRO
    slots = tokens.shape[1]
    lengths = jnp.where(bucket_ids == 0, slots, slots - slots // 16) // 2
    valid = jnp.where(jnp.arange(local) < group_counts[0], lengths, 0).astype(jnp.int32)
    biases = (
        modulation_bias.astype(jnp.float32),
        query_value_bias.astype(jnp.float32),
        output_bias.astype(jnp.float32),
        expand_bias.astype(jnp.float32),
        shrink_bias.astype(jnp.float32),
    )
    block_parts = []
    grad_parts = []
    weight_sums = None
    bias_sums = None
    for micro in range(MICRO):
        full = gather_weights(
            modulation_weight, input_weight, output_weight, expand_weight, shrink_weight
        )
        begin = micro * per_micro
        finish = begin + per_micro
        block_mb, grad_mb, terms, bias_terms, silu_cond, grad_mod_low = run_micro(
            tokens[begin:finish],
            conditioning[begin:finish],
            keep_order[begin:finish],
            valid[begin:finish],
            cotangent[begin:finish],
            full,
            biases,
        )
        block_parts.append(block_mb)
        grad_parts.append(grad_mb)
        mod_term = jnp.einsum(
            "bd,be->de", silu_cond, grad_mod_low, preferred_element_type=jnp.float32
        )
        terms = (mod_term,) + tuple(terms)
        terms = scatter_every(terms)
        if weight_sums is None:
            weight_sums = tuple(terms)
            bias_sums = bias_terms
        else:
            weight_sums = tuple((left + right for left, right in zip(weight_sums, terms)))
            bias_sums = tuple((left + right for left, right in zip(bias_sums, bias_terms)))
    bias_sums = lax.psum(
        (bias_sums[0], bias_sums[1], bias_sums[2], bias_sums[3], bias_sums[4]), "dp"
    )
    return (
        jnp.concatenate(block_parts, axis=0),
        jnp.concatenate(grad_parts, axis=0),
        weight_sums[0],
        bias_sums[0],
        weight_sums[1],
        bias_sums[1],
        weight_sums[2],
        bias_sums[2],
        weight_sums[3],
        bias_sums[3],
        weight_sums[4],
        bias_sums[4],
    )


def solution(mesh):
    in_specs = (
        P("dp", None, None),
        P("dp", None),
        P("dp"),
        P("dp", None),
        P("dp"),
        P("dp", None, None),
        P("dp", None),
        P(),
        P(None, "dp", "mp"),
        P(None, "mp"),
        P("mp", "dp"),
        P(),
        P("dp", "mp"),
        P("mp"),
        P("mp", "dp"),
        P(),
    )
    out_specs = (
        P("dp", None, None),
        P("dp", None, None),
        P("dp", None),
        P(),
        P(None, "dp", "mp"),
        P(None, "mp"),
        P("mp", "dp"),
        P(),
        P("dp", "mp"),
        P("mp"),
        P("mp", "dp"),
        P(),
    )
    return jax.shard_map(body, mesh=mesh, in_specs=in_specs, out_specs=out_specs, check_vma=False)
```

profile of v0, /device:TPU:0, one launch (start us, length us, event | category | flops | bytes accessed | tf_op | source)
XLA Modules:
  0.0 1631.6 jit_solution(14965664791636846735)
XLA Ops:
  13.0 3.8 gather_fusion
  18.7 115.8 %all-gather.14.cloned.1.call-done = bf16[1152,6912]{1,0:T(8,128)(2,1)} async-done(((bf16[72,6912]{1,0:T(8,128)(2,1)}), bf16[1152,6912]{1,0:T(8,128)(2,1)}) %all-gather.14.cloned.1.call-update) | async-done | bytes 15925264 | tf_op jit(solution)/shard_map/all_gather | solution.py:32
  134.5 7.7 convolution_add_fusion.2
  142.3 44.3 %all-gather.16.cloned.1.call-done = bf16[3,1152,576]{2,1,0:T(8,128)(2,1)} async-done(((bf16[3,72,576]{2,1,0:T(8,128)(2,1)}), bf16[3,1152,576]{2,1,0:T(8,128)(2,1)}) %all-gather.16.cloned.1.call-update) | async-done | bytes 3981328 | tf_op jit(solution)/shard_map/all_gather | solution.py:33
  186.6 4.7 fusion.64
  193.7 33.0 %all-gather.18.cloned.1.call-done = bf16[576,1152]{0,1:T(8,128)(2,1)} async-done(((bf16[576,72]{0,1:T(8,128)(2,1)}), bf16[576,1152]{0,1:T(8,128)(2,1)}) %all-gather.18.cloned.1.call-update) | async-done | bytes 1327120 | tf_op jit(solution)/shard_map/all_gather | solution.py:34
  226.7 3.0 fusion.74
  229.8 20.7 %reduce-scatter.15.cloned.1.call-done = f32[2,128,576]{1,2,0:T(8,128)} async-done(((f32[2,128,1152]{1,2,0:T(8,128)}), f32[2,128,576]{1,2,0:T(8,128)}) %reduce-scatter.15.cloned.1.call-update) | async-done | bytes 589840 | tf_op jit(solution)/shard_map/reduce_scatter | solution.py:26
  253.2 3.0 gather_fusion.1
  258.8 3.8 gather_fusion.2
  267.5 7.3 all-gather.20.cloned.1.call-done
  278.5 54.9 %all-gather.22.cloned.1.call-done = bf16[1152,2304]{1,0:T(8,128)(2,1)} async-done(((bf16[72,2304]{1,0:T(8,128)(2,1)}), bf16[1152,2304]{1,0:T(8,128)(2,1)}) %all-gather.22.cloned.1.call-update) | async-done | bytes 5308432 | tf_op jit(solution)/shard_map/all_gather | solution.py:35
  333.4 5.8 fusion.27
  339.2 51.5 %all-gather.24.cloned.1.call-done = bf16[2304,1152]{0,1:T(8,128)(2,1)} async-done(((bf16[2304,72]{0,1:T(8,128)(2,1)}), bf16[2304,1152]{0,1:T(8,128)(2,1)}) %all-gather.24.cloned.1.call-update) | async-done | bytes 5308432 | tf_op jit(solution)/shard_map/all_gather | solution.py:36
  390.8 7.1 fusion.194
  398.9 2.6 fusion.13
  401.8 8.7 convolution_add_fusion.1
  413.9 4.7 fusion.67
  424.0 3.8 gather_fusion.3
  431.2 15.4 reduce-scatter.19.cloned.1.call-done
  447.8 23.2 %all-gather.32.cloned.1.call-done = f32[2,128,1152]{1,2,0:T(8,128)} async-done(((f32[2,128,576]{1,2,0:T(8,128)}), f32[2,128,1152]{1,2,0:T(8,128)}) %all-gather.32.cloned.1.call-update) | async-done | bytes 1179664 | tf_op jit(solution)/shard_map/all_gather | solution.py:27
  475.0 20.4 %all-gather.28.cloned.1.call-done = f32[2,128,1152]{1,2,0:T(8,128)} async-done(((f32[2,128,576]{1,2,0:T(8,128)}), f32[2,128,1152]{1,2,0:T(8,128)}) %all-gather.28.cloned.1.call-update) | async-done | bytes 1179664 | tf_op jit(solution)/shard_map/all_gather | solution.py:27
  495.4 5.5 multiply_reduce_fusion.9
  501.7 4.6 fusion.30
  506.4 7.2 fusion.195
  514.6 2.6 fusion.11
  517.3 21.9 %reduce-scatter.27.cloned.1.call-done = f32[2,128,576]{1,2,0:T(8,128)} async-done(((f32[2,128,1152]{1,2,0:T(8,128)}), f32[2,128,576]{1,2,0:T(8,128)}) %reduce-scatter.27.cloned.1.call-update) | async-done | bytes 589840 | tf_op jit(solution)/shard_map/reduce_scatter | solution.py:26
  539.2 5.9 fusion.9
  546.1 3.1 fusion.88
  553.8 4.6 fusion.37
  559.8 5.9 fusion.7
  568.4 2.4 multiply_reduce_fusion
  579.4 4.6 fusion.34
  584.1 3.3 reduce-scatter.17.cloned.1.call-done
  587.5 23.9 %reduce-scatter.25.cloned.1.call-done = f32[2,128,576]{1,2,0:T(8,128)} async-done(((f32[2,128,1152]{1,2,0:T(8,128)}), f32[2,128,576]{1,2,0:T(8,128)}) %reduce-scatter.25.cloned.1.call-update) | async-done | bytes 589840 | tf_op jit(solution)/shard_map/reduce_scatter | solution.py:26
  611.4 24.4 %reduce-scatter.21.cloned.1.call-done = f32[2,128,576]{1,2,0:T(8,128)} async-done(((f32[2,128,1152]{1,2,0:T(8,128)}), f32[2,128,576]{1,2,0:T(8,128)}) %reduce-scatter.21.cloned.1.call-update) | async-done | bytes 589840 | tf_op jit(solution)/shard_map/reduce_scatter | solution.py:26
  635.9 23.9 %reduce-scatter.29.cloned.1.call-done = f32[2,128,576]{1,2,0:T(8,128)} async-done(((f32[2,128,1152]{1,2,0:T(8,128)}), f32[2,128,576]{1,2,0:T(8,128)}) %reduce-scatter.29.cloned.1.call-update) | async-done | bytes 589840 | tf_op jit(solution)/shard_map/reduce_scatter | solution.py:26
  660.1 3.1 fusion.136
  663.3 4.5 fusion.2
  667.9 13.8 copy.156
  681.8 2.2 convolution_bitcast_fusion.5
  684.1 2.6 fusion.33
  686.8 3.8 convolution_bitcast_fusion.1
  690.7 5.4 fusion
  696.7 3.4 convolution_bitcast_fusion.3
  700.2 5.2 fusion.1
  708.3 5.0 fusion.80
  714.1 2.3 fusion.96
  717.3 12.5 fusion.178
  729.8 2.8 all-gather.30.cloned.1.call-done
  732.5 24.4 %all-gather.38.cloned.1.call-done = f32[2,128,1152]{1,2,0:T(8,128)} async-done(((f32[2,128,576]{1,2,0:T(8,128)}), f32[2,128,1152]{1,2,0:T(8,128)}) %all-gather.38.cloned.1.call-update) | async-done | bytes 1179664 | tf_op jit(solution)/shard_map/all_gather | solution.py:27
  757.0 4.7 fusion.82
  763.7 25.0 %convolution_add_fusion = f32[1152,6912]{1,0:T(8,128)} fusion(f32[1152,6912]{1,0:T(8,128)} %fusion.178, bf16[2,6912]{1,0:T(2,128)(2,1)S(1)} %bitcast.353, bf16[4,1152]{1,0:T(4,128)(2,1)S(1)} %copy-done.78), kind=kOutput, calls=%fused_computation.8 | convolution fusion | flops 39826944 | bytes 63733248 | tf_op jit(solution)/shard_map/bd,be->de/dot_general | solution.py:303
  798.2 17.7 %scatter_fusion.2 = bf16[2,256,1152]{2,1,0:T(8,128)(2,1)S(1)} fusion(bf16[2,256,1152]{2,1,0:T(8,128)(2,1)S(1)} %copy-done.7, s32[256]{0:T(256)S(1)} %copy-done.10, bf16[256,1152]{1,0:T(8,128)(2,1)S(1)} %bitcast.322), kind=kCustom, calls=%fused_computation.6 | custom fusion | bytes 1771520 | tf_op jit(solution)/shard_map/scatter | solution.py:229
  816.0 26.8 %scatter_fusion = bf16[2,256,1152]{2,1,0:T(8,128)(2,1)S(1)} fusion(bf16[2,256,1152]{2,1,0:T(8,128)(2,1)S(1)} %copy-done.3, s32[256]{0:T(256)S(1)} %copy-done.10, bf16[256,1152]{1,0:T(8,128)(2,1)} %bitcast.321), kind=kCustom, calls=%fused_computation.4 | custom fusion | bytes 1771520 | tf_op jit(solution)/shard_map/scatter | solution.py:132
  852.4 26.6 %scatter_fusion.3 = bf16[2,256,1152]{2,1,0:T(8,128)(2,1)S(1)} fusion(bf16[2,256,1152]{2,1,0:T(8,128)(2,1)S(1)} %copy-done.5, s32[256]{0:T(256)S(1)} %copy-done.9, bf16[256,1152]{1,0:T(8,128)(2,1)} %bitcast.319), kind=kCustom, calls=%fused_computation.7 | custom fusion | bytes 1771520 | tf_op jit(solution)/shard_map/scatter | solution.py:229
  879.0 26.6 %scatter_fusion.1 = bf16[2,256,1152]{2,1,0:T(8,128)(2,1)S(1)} fusion(bf16[2,256,1152]{2,1,0:T(8,128)(2,1)S(1)} %copy-done.1, s32[256]{0:T(256)S(1)} %copy-done.9, bf16[256,1152]{1,0:T(8,128)(2,1)} %bitcast.320), kind=kCustom, calls=%fused_computation.5 | custom fusion | bytes 1771520 | tf_op jit(solution)/shard_map/scatter | solution.py:132
  906.9 63.9 %all-reduce.2 = (f32[6912]{0:T(1024)}, f32[2,576]{1,0:T(2,128)}, f32[1152]{0:T(1024)}, f32[2304]{0:T(1024)}, f32[1152]{0:T(1024)}) all-reduce(f32[6912]{0:T(1024)} %add.447, f32[2,576]{1,0:T(2,128)} %add.449, f32[1152]{0:T(1024)} %add.451, f32[2304]{0:T(1024)S(1)} %copy-done.118, f32[1152]{0:T(1024)} %add.455), channel_id=1, replica_groups=mesh['dp'=16,'mp'=2] {'dp'}, use_global_device_ids=true, to_apply=%region_50.52 | all-reduce | flops 12672 | bytes 101376 | tf_op jit(solution)/shard_map/psum | solution.py:314
  970.8 2.9 pad_maximum_fusion.1
  975.3 6.7 all-reduce.5.cloned.1.call-done
  984.1 67.8 %reduce-scatter.37.cloned.1.call-done = f32[576,72]{0,1:T(8,128)} async-done(((f32[576,1152]{0,1:T(8,128)}), f32[576,72]{0,1:T(8,128)}) %reduce-scatter.37.cloned.1.call-update) | async-done | bytes 165904
  1052.0 123.8 %reduce-scatter.35.cloned.1.call-done = f32[2304,72]{0,1:T(8,128)} async-done(((f32[2304,1152]{0,1:T(8,128)}), f32[2304,72]{0,1:T(8,128)}) %reduce-scatter.35.cloned.1.call-update) | async-done | bytes 663568 | tf_op jit(solution)/shard_map/reduce_scatter | solution.py:46
  1175.8 124.6 %reduce-scatter.33.cloned.1.call-done = f32[72,2304]{1,0:T(8,128)} async-done(((f32[1152,2304]{1,0:T(8,128)}), f32[72,2304]{1,0:T(8,128)}) %reduce-scatter.33.cloned.1.call-update) | async-done | bytes 663568 | tf_op jit(solution)/shard_map/reduce_scatter | solution.py:45
  1300.4 324.4 %reduce-scatter.31.cloned.1.call-done = f32[72,6912]{1,0:T(8,128)} async-done(((f32[1152,6912]{1,0:T(8,128)}), f32[72,6912]{1,0:T(8,128)}) %reduce-scatter.31.cloned.1.call-update) | async-done | bytes 1990672 | tf_op jit(solution)/shard_map/reduce_scatter | solution.py:42
  (549 shorter events, 91.9 us)
Async XLA Ops:
  7.2 127.3 %all-gather.14.cloned.1.call-start = ((), (), s32[]{:S(2)}) async-start(), calls=%async_computation.12 | async-start | bytes 16920576 | tf_op jit(solution)/shard_map/all_gather | solution.py:32
  8.0 178.7 %all-gather.16.cloned.1.call-start = ((), (), s32[]{:S(2)}) async-start(), calls=%async_computation.13 | async-start | bytes 4700160 | tf_op jit(solution)/shard_map/all_gather | solution.py:33
  8.7 218.0 %all-gather.18.cloned.1.call-start = ((), (), s32[]{:S(2)}) async-start(), calls=%async_computation.14 | async-start | bytes 1566720 | tf_op jit(solution)/shard_map/all_gather | solution.py:34
  9.4 241.0 %reduce-scatter.15.cloned.1.call-start = ((), (), s32[]{:S(2)}) async-start(), calls=%async_computation.15 | async-start | bytes 1769472 | tf_op jit(solution)/shard_map/reduce_scatter | solution.py:26
  9.5 177.1 %copy-start.104 = (pred[2,128]{1,0:T(4,128)(4,1)}, pred[2,128]{1,0:T(4,128)(4,1)S(1)}, u32[]{:S(2)}) copy-start(pred[2,128]{1,0:T(4,128)(4,1)S(1)} %get-tuple-element.124) | copy-start | bytes 772
  9.5 254.7 %copy-start.110 = (pred[2,128]{1,0:T(4,128)(4,1)}, pred[2,128]{1,0:T(4,128)(4,1)S(1)}, u32[]{:S(2)}) copy-start(pred[2,128]{1,0:T(4,128)(4,1)S(1)} %get-tuple-element.125) | copy-start | bytes 772
  11.0 180.6 %copy-start.148 = (pred[2,128]{1,0:T(4,128)(4,1)}, pred[2,128]{1,0:T(4,128)(4,1)S(1)}, u32[]{:S(2)}) copy-start(pred[2,128]{1,0:T(4,128)(4,1)S(1)} %iota_compare_fusion.2) | copy-start | bytes 772
  11.1 181.8 %copy-start.124 = (f32[8,72]{1,0:T(8,128)}, f32[8,72]{1,0:T(8,128)S(1)}, u32[]{:S(2)}) copy-start(f32[8,72]{1,0:T(8,128)S(1)} %add.391) | copy-start | bytes 6916
  11.1 180.4 %copy-start.93 = (f32[8,72]{1,0:T(8,128)}, f32[8,72]{1,0:T(8,128)S(1)}, u32[]{:S(2)}) copy-start(f32[8,72]{1,0:T(8,128)S(1)} %add.394) | copy-start | bytes 6916
  11.2 123.3 %copy-start.76 = (f32[6912]{0:T(1024)}, f32[6912]{0:T(1024)S(1)}, u32[]{:S(2)}) copy-start(f32[6912]{0:T(1024)S(1)} %convert_element_type.170) | copy-start | bytes 82948
  13.0 240.2 %copy-start = (bf16[2,256,1152]{2,1,0:T(8,128)(2,1)}, bf16[2,256,1152]{2,1,0:T(8,128)(2,1)S(1)}, u32[]{:S(2)}) copy-start(bf16[2,256,1152]{2,1,0:T(8,128)(2,1)S(1)} %get-tuple-element.99) | copy-start | bytes 3538948
  16.8 117.7 %copy-start.77 = (bf16[4,1152]{1,0:T(4,128)(2,1)S(1)}, bf16[4,1152]{1,0:T(4,128)(2,1)}, u32[]{:S(2)}) copy-start(bf16[4,1152]{1,0:T(4,128)(2,1)} %param.19) | copy-start | bytes 27652
  18.2 168.4 %copy-start.13 = (bf16[2,128,1152]{1,2,0:T(8,128)(2,1)}, bf16[2,128,1152]{1,2,0:T(8,128)(2,1)S(1)}, u32[]{:S(2)}) copy-start(bf16[2,128,1152]{1,2,0:T(8,128)(2,1)S(1)} %copy.124) | copy-start | bytes 1769476
  18.4 168.2 %copy-start.139 = (f32[2,128]{1,0:T(2,128)}, f32[2,128]{1,0:T(2,128)S(1)}, u32[]{:S(2)}) copy-start(f32[2,128]{1,0:T(2,128)S(1)} %broadcast_multiply_fusion.3) | copy-start | bytes 3076
  18.6 123.5 %copy-start.170 = (f32[2,128]{1,0:T(2,128)}, f32[2,128]{1,0:T(2,128)S(1)}, u32[]{:S(2)}) copy-start(f32[2,128]{1,0:T(2,128)S(1)} %fusion.108) | copy-start | bytes 3076
  18.7 168.0 %copy-start.157 = (f32[2,128]{1,0:T(2,128)}, f32[2,128]{1,0:T(2,128)S(1)}, u32[]{:S(2)}) copy-start(f32[2,128]{1,0:T(2,128)S(1)} %fusion.164) | copy-start | bytes 3076
  142.3 49.0 %copy-start.119 = (f32[2,1,1,1152]{3,0,1,2:T(2,128)}, f32[2,1,1,1152]{3,0,1,2:T(2,128)S(1)}, u32[]{:S(2)}) copy-start(f32[2,1,1,1152]{3,0,1,2:T(2,128)S(1)} %copy.215) | copy-start | bytes 27652
  142.3 49.0 %copy-start.79 = (f32[2,1,1,1152]{3,0,1,2:T(2,128)}, f32[2,1,1,1152]{3,0,1,2:T(2,128)S(1)}, u32[]{:S(2)}) copy-start(f32[2,1,1,1152]{3,0,1,2:T(2,128)S(1)} %copy.216) | copy-start | bytes 27652
  193.6 36.0 %copy-start.69 = (bf16[2,8,72,128]{3,2,1,0:T(8,128)(2,1)}, bf16[2,8,72,128]{3,2,1,0:T(8,128)(2,1)S(1)}, u32[]{:S(2)}) copy-start(bf16[2,8,72,128]{3,2,1,0:T(8,128)(2,1)S(1)} %convolution_convert_fusion.1) | copy-start | bytes 884740
  229.7 22.3 %copy-start.180 = (bf16[1152]{0:T(1024)(128)(2,1)S(1)}, bf16[1152]{0:T(1024)(128)(2,1)}, u32[]{:S(2)}) copy-start(bf16[1152]{0:T(1024)(128)(2,1)} %param.29) | copy-start | bytes 6916
  229.7 22.9 %copy-start.177 = (bf16[2304]{0:T(1024)(128)(2,1)S(1)}, bf16[2304]{0:T(1024)(128)(2,1)}, u32[]{:S(2)}) copy-start(bf16[2304]{0:T(1024)(128)(2,1)} %param.31) | copy-start | bytes 13828
  229.7 45.0 %all-gather.20.cloned.1.call-start = ((), (), s32[]{:S(2)}) async-start(), calls=%async_computation.16 | async-start | bytes 1769472 | tf_op jit(solution)/shard_map/all_gather | solution.py:27
  250.5 82.9 %all-gather.22.cloned.1.call-start = ((), (), s32[]{:S(2)}) async-start(), calls=%async_computation.17 | async-start | bytes 5640192 | tf_op jit(solution)/shard_map/all_gather | solution.py:35
  251.0 139.7 %all-gather.24.cloned.1.call-start = ((), (), s32[]{:S(2)}) async-start(), calls=%async_computation.18 | async-start | bytes 5640192 | tf_op jit(solution)/shard_map/all_gather | solution.py:36
  251.8 171.6 %reduce-scatter.23.cloned.1.call-start = ((), (), s32[]{:S(2)}) async-start(), calls=%async_computation.25 | async-start | bytes 1769472 | tf_op jit(solution)/shard_map/reduce_scatter | solution.py:26
  258.8 165.2 %copy-start.4 = (bf16[2,256,1152]{2,1,0:T(8,128)(2,1)}, bf16[2,256,1152]{2,1,0:T(8,128)(2,1)S(1)}, u32[]{:S(2)}) copy-start(bf16[2,256,1152]{2,1,0:T(8,128)(2,1)S(1)} %get-tuple-element.97) | copy-start | bytes 3538948
  264.1 126.7 %copy-start.31 = (bf16[2,128,1152]{1,2,0:T(8,128)(2,1)}, bf16[2,128,1152]{1,2,0:T(8,128)(2,1)S(1)}, u32[]{:S(2)}) copy-start(bf16[2,128,1152]{1,2,0:T(8,128)(2,1)S(1)} %copy.134) | copy-start | bytes 1769476
  401.6 45.1 %reduce-scatter.19.cloned.1.call-start = ((), (), s32[]{:S(2)}) async-start(), calls=%async_computation.21 | async-start | bytes 1769472 | tf_op jit(solution)/shard_map/reduce_scatter | solution.py:26
  423.3 47.6 %all-gather.32.cloned.1.call-start = ((), (), s32[]{:S(2)}) async-start(), calls=%async_computation.26 | async-start | bytes 1769472 | tf_op jit(solution)/shard_map/all_gather | solution.py:27
  423.9 71.4 %all-gather.28.cloned.1.call-start = ((), (), s32[]{:S(2)}) async-start(), calls=%async_computation.22 | async-start | bytes 1769472 | tf_op jit(solution)/shard_map/all_gather | solution.py:27
  427.8 19.3 %copy-start.134 = (f32[2,1,1,1152]{3,1,0,2:T(1,128)S(1)}, f32[2,1,1,1152]{3,1,0,2:T(1,128)}, u32[]{:S(2)}) copy-start(f32[2,1,1,1152]{3,1,0,2:T(1,128)} %get-tuple-element.114) | copy-start | bytes 27652
  427.8 43.1 %copy-start.99 = (f32[2,128]{1,0:T(2,128)S(1)}, f32[2,128]{1,0:T(2,128)}, u32[]{:S(2)}) copy-start(f32[2,128]{1,0:T(2,128)} %copy-done.98) | copy-start | bytes 3076
  446.7 92.5 %reduce-scatter.27.cloned.1.call-start = ((), (), s32[]{:S(2)}) async-start(), calls=%async_computation.29 | async-start | bytes 1769472 | tf_op jit(solution)/shard_map/reduce_scatter | solution.py:26
  447.7 24.9 %copy-start.174 = (f32[2,128]{1,0:T(2,128)S(1)}, f32[2,128]{1,0:T(2,128)}, u32[]{:S(2)}) copy-start(f32[2,128]{1,0:T(2,128)} %copy-done.173) | copy-start | bytes 3076
  447.8 25.0 %copy-start.117 = (f32[2,128]{1,0:T(2,128)S(1)}, f32[2,128]{1,0:T(2,128)}, u32[]{:S(2)}) copy-start(f32[2,128]{1,0:T(2,128)} %fusion.165) | copy-start | bytes 3076
  517.2 48.6 %all-gather.36.cloned.1.call-start = ((), (), s32[]{:S(2)}) async-start(), calls=%async_computation.30 | async-start | bytes 1769472 | tf_op jit(solution)/shard_map/all_gather | solution.py:27
  539.2 48.2 %reduce-scatter.17.cloned.1.call-start = ((), (), s32[]{:S(2)}) async-start(), calls=%async_computation.19 | async-start | bytes 1769472 | tf_op jit(solution)/shard_map/reduce_scatter | solution.py:26
  545.2 66.2 %reduce-scatter.25.cloned.1.call-start = ((), (), s32[]{:S(2)}) async-start(), calls=%async_computation.27 | async-start | bytes 1769472 | tf_op jit(solution)/shard_map/reduce_scatter | solution.py:26
  558.4 77.4 %reduce-scatter.21.cloned.1.call-start = ((), (), s32[]{:S(2)}) async-start(), calls=%async_computation.23 | async-start | bytes 1769472 | tf_op jit(solution)/shard_map/reduce_scatter | solution.py:26
  565.7 94.0 %reduce-scatter.29.cloned.1.call-start = ((), (), s32[]{:S(2)}) async-start(), calls=%async_computation.31 | async-start | bytes 1769472 | tf_op jit(solution)/shard_map/reduce_scatter | solution.py:26
  584.0 123.2 %all-gather.26.cloned.1.call-start = ((), (), s32[]{:S(2)}) async-start(), calls=%async_computation.20 | async-start | bytes 1769472 | tf_op jit(solution)/shard_map/all_gather | solution.py:27
  587.4 72.7 %copy-start.105 = (pred[2,128]{1,0:T(4,128)(4,1)S(1)}, pred[2,128]{1,0:T(4,128)(4,1)}, u32[]{:S(2)}) copy-start(pred[2,128]{1,0:T(4,128)(4,1)} %copy-done.104) | copy-start | bytes 772
  587.4 120.9 %all-gather.34.cloned.1.call-start = ((), (), s32[]{:S(2)}) async-start(), calls=%async_computation.28 | async-start | bytes 1769472 | tf_op jit(solution)/shard_map/all_gather | solution.py:27
  611.4 121.2 %all-gather.30.cloned.1.call-start = ((), (), s32[]{:S(2)}) async-start(), calls=%async_computation.24 | async-start | bytes 1769472 | tf_op jit(solution)/shard_map/all_gather | solution.py:27
  635.8 121.1 %all-gather.38.cloned.1.call-start = ((), (), s32[]{:S(2)}) async-start(), calls=%async_computation.32 | async-start | bytes 1769472 | tf_op jit(solution)/shard_map/all_gather | solution.py:27
  659.8 322.3 %all-reduce.5.cloned.1.call-start = ((), (), s32[]{:S(2)}) async-start(), calls=%async_computation.36 | async-start | bytes 23592960
  681.7 370.3 %reduce-scatter.37.cloned.1.call-start = ((), (), s32[]{:S(2)}) async-start(), calls=%async_computation.37 | async-start | bytes 3133440
  686.7 489.1 %reduce-scatter.35.cloned.1.call-start = ((), (), s32[]{:S(2)}) async-start(), calls=%async_computation.35 | async-start | bytes 11280384 | tf_op jit(solution)/shard_map/reduce_scatter | solution.py:46
  696.1 604.3 %reduce-scatter.33.cloned.1.call-start = ((), (), s32[]{:S(2)}) async-start(), calls=%async_computation.34 | async-start | bytes 11280384 | tf_op jit(solution)/shard_map/reduce_scatter | solution.py:45
  705.4 919.4 %reduce-scatter.31.cloned.1.call-start = ((), (), s32[]{:S(2)}) async-start(), calls=%async_computation.33 | async-start | bytes 33841152 | tf_op jit(solution)/shard_map/reduce_scatter | solution.py:42
  717.2 39.7 %copy-start.29 = (bf16[2,128,1152]{1,2,0:T(8,128)(2,1)S(1)}, bf16[2,128,1152]{1,2,0:T(8,128)(2,1)}, u32[]{:S(2)}) copy-start(bf16[2,128,1152]{1,2,0:T(8,128)(2,1)} %copy.144) | copy-start | bytes 1769476
  717.2 39.7 %copy-start.83 = (f32[2,1,1,1152]{3,0,1,2:T(2,128)S(1)}, f32[2,1,1,1152]{3,0,1,2:T(2,128)}, u32[]{:S(2)}) copy-start(f32[2,1,1,1152]{3,0,1,2:T(2,128)} %copy-done.81) | copy-start | bytes 27652
  717.2 39.7 %copy-start.92 = (f32[2,1,1,1152]{3,0,1,2:T(2,128)S(1)}, f32[2,1,1,1152]{3,0,1,2:T(2,128)}, u32[]{:S(2)}) copy-start(f32[2,1,1,1152]{3,0,1,2:T(2,128)} %copy.210) | copy-start | bytes 27652
  717.2 39.7 %copy-start.103 = (f32[1152]{0:T(1024)S(1)}, f32[1152]{0:T(1024)}, u32[]{:S(2)}) copy-start(f32[1152]{0:T(1024)} %convert_element_type.183) | copy-start | bytes 13828
  717.2 39.7 %copy-start.115 = (pred[2,128]{1,0:T(4,128)(4,1)S(1)}, pred[2,128]{1,0:T(4,128)(4,1)}, u32[]{:S(2)}) copy-start(pred[2,128]{1,0:T(4,128)(4,1)} %copy-done.110) | copy-start | bytes 772
  717.3 39.7 %copy-start.143 = (f32[2,128]{1,0:T(2,128)S(1)}, f32[2,128]{1,0:T(2,128)}, u32[]{:S(2)}) copy-start(f32[2,128]{1,0:T(2,128)} %copy-done.141) | copy-start | bytes 3076
  717.3 39.7 %copy-start.155 = (pred[2,128]{1,0:T(4,128)(4,1)S(1)}, pred[2,128]{1,0:T(4,128)(4,1)}, u32[]{:S(2)}) copy-start(pred[2,128]{1,0:T(4,128)(4,1)} %iota_compare_fusion.1) | copy-start | bytes 772
  729.8 31.9 %copy-start.172 = (f32[2,128]{1,0:T(2,128)S(1)}, f32[2,128]{1,0:T(2,128)}, u32[]{:S(2)}) copy-start(f32[2,128]{1,0:T(2,128)} %copy-done.171) | copy-start | bytes 3076
  729.8 31.9 %copy-start.160 = (f32[2,128]{1,0:T(2,128)S(1)}, f32[2,128]{1,0:T(2,128)}, u32[]{:S(2)}) copy-start(f32[2,128]{1,0:T(2,128)} %fusion.166) | copy-start | bytes 3076
  816.0 26.9 %copy-start.8 = (bf16[2,256,1152]{2,1,0:T(8,128)(2,1)}, bf16[2,256,1152]{2,1,0:T(8,128)(2,1)S(1)}, u32[]{:S(2)}) copy-start(bf16[2,256,1152]{2,1,0:T(8,128)(2,1)S(1)} %scatter_fusion.2) | copy-start | bytes 3538948
  816.0 26.8 %copy-start.145 = (f32[1152]{0:T(1024)S(1)}, f32[1152]{0:T(1024)}, u32[]{:S(2)}) copy-start(f32[1152]{0:T(1024)} %get-tuple-element.69) | copy-start | bytes 13828
  816.0 28.1 %copy-start.45 = (f32[2,8,72,128]{3,2,1,0:T(8,128)S(1)}, f32[2,8,72,128]{3,2,1,0:T(8,128)}, u32[]{:S(2)}) copy-start(f32[2,8,72,128]{3,2,1,0:T(8,128)} %copy-done.43) | copy-start | bytes 1769476
  852.4 26.6 %copy-start.1 = (bf16[2,256,1152]{2,1,0:T(8,128)(2,1)S(1)}, bf16[2,256,1152]{2,1,0:T(8,128)(2,1)}, u32[]{:S(2)}) copy-start(bf16[2,256,1152]{2,1,0:T(8,128)(2,1)} %copy-done) | copy-start | bytes 3538948
  879.0 27.9 %copy-start.118 = (f32[2304]{0:T(1024)S(1)}, f32[2304]{0:T(1024)}, u32[]{:S(2)}) copy-start(f32[2304]{0:T(1024)} %add.453) | copy-start | bytes 27652
  (148 other events, 437.5 us)
Sparse Core Ops, SparseCore 0:
  10.2 124.2 all-gather.13
  136.7 49.9 all-gather.15
  188.8 37.8 all-gather.17
  229.8 20.5 reduce-scatter.14
  251.9 22.7 all-gather.19
  277.0 56.3 all-gather.21
  335.8 54.9 all-gather.23
  401.7 20.3 reduce-scatter.22
  424.9 21.7 reduce-scatter.18
  448.1 22.7 all-gather.31
  472.6 22.7 all-gather.27
  517.4 21.7 reduce-scatter.26
  540.7 22.7 all-gather.35
  565.6 21.7 reduce-scatter.16
  589.6 21.7 reduce-scatter.24
  614.0 21.7 reduce-scatter.20
  638.0 21.7 reduce-scatter.28
  661.2 22.7 all-gather.25
  685.5 22.7 all-gather.33
  709.7 22.7 all-gather.29
  734.1 22.7 all-gather.37
  760.6 221.4 all-reduce.4
  986.6 65.3 reduce-scatter.36
  1056.5 119.2 reduce-scatter.34
  1180.4 119.9 reduce-scatter.32
  1305.1 319.6 reduce-scatter.30
where the time goes:
time: 1640 us; the launch traced here: 1630 us
  waiting for transfers between devices  1160 us (71%)
  local copies, waits for them, and re-layouts  166 us (10%)
  matrix products  159 us (10%)
  blocking collectives  63.9 us (4%)
  other arithmetic  58.5 us (4%)
  between operations  17.8 us (1%)
    reduce_scatter x1, waiting for transfers between devices, scatter_every(): lax.psum_scatter(terms[0], 'dp', scatter_dimension=0, tiled=True)  324 us
    reduce_scatter x8, waiting for transfers between devices, model_total_sum(): lax.psum_scatter(partial_value, 'mp', scatter_dimension=2, tiled=True)  133 us
    reduce_scatter x1, waiting for transfers between devices, scatter_every(): lax.psum_scatter(terms[3], 'dp', scatter_dimension=0, tiled=True)  125 us
    reduce_scatter x1, waiting for transfers between devices, scatter_every(): lax.psum_scatter(terms[4], 'dp', scatter_dimension=1, tiled=True)  124 us
    all_gather x1, waiting for transfers between devices, gather_weights(): lax.all_gather(modulation_weight, 'dp', axis=0, tiled=True)  116 us
    all_gather x8, waiting for transfers between devices, model_total_sum(): return lax.all_gather(share, 'mp', axis=2, tiled=True)  79.1 us
    unnamed x28, waiting for transfers between devices  78.7 us
    psum x1, blocking collectives, body(): lax.psum((bias_sums[0], bias_sums[1], bias_sums[2], bias_sums[3], bias_su...  63.9 us
  transfers between devices with their start and end apart: 26, of which 23 were waited for; matrix products, arithmetic and copies ran while one was open for 21% of the time, Pallas kernels for 0%

commit v1 on v0

--- a/solution.py
+++ b/solution.py
@@ -8,6 +8,18 @@
 EPSILON = 1e-06
 
 
+def doubled_up(shard, axis, dim):
+    ways, here = (lax.axis_size(axis), lax.axis_index(axis))
+    grown, reach = (shard, 1)
+    while reach < ways:
+        theirs = lax.ppermute(grown, axis, [(d, d ^ reach) for d in range(ways)])
+        mine_first = jnp.concatenate([grown, theirs], axis=dim)
+        theirs_first = jnp.concatenate([theirs, grown], axis=dim)
+        grown = jnp.where(here & reach == 0, mine_first, theirs_first)
+        reach = 2 * reach
+    return grown
+
+
 def normalize(rows):
     center = rows - jnp.mean(rows, axis=-1, keepdims=True)
     spread = jnp.mean(center * center, axis=-1, keepdims=True)
@@ -24,7 +36,7 @@
 
 def model_total_sum(partial_value):
     share = lax.psum_scatter(partial_value, "mp", scatter_dimension=2, tiled=True)
-    return lax.all_gather(share, "mp", axis=2, tiled=True)
+    return doubled_up(share, "mp", 2)
 
 
 def gather_weights(modulation_weight, input_weight, output_weight, expand_weight, shrink_weight):

time: 1640 us -> 1460 us (0.89)
  waiting for transfers between devices: 1160 us -> 961 us
    reduce_scatter x8, waiting for transfers between devices: 133 us -> 45.3 us  [model_total_sum(): lax.psum_scatter(partial_value, 'mp', scatter_dimension=2, tiled=True)]
    all_gather x8 -> x0, waiting for transfers between devices: 79.1 us -> none  [model_total_sum(): return lax.all_gather(share, 'mp', axis=2, tiled=True)]
    unnamed x28 -> x20, waiting for transfers between devices: 78.7 us -> 7.05 us
    ppermute x0 -> x8, waiting for transfers between devices: none -> 58.1 us  [doubled_up(): theirs = lax.ppermute(grown, axis, [(d, d ^ reach) for d in range(ways)])]
    all_gather x1, waiting for transfers between devices: 54.9 us -> 37.3 us  [gather_weights(): lax.all_gather(expand_weight, 'dp', axis=0, tiled=True)]
  transfers between devices with their start and end apart: 26 -> 26, of which waited for: 23 -> 19; matrix products, arithmetic and copies ran while one was open for 21% -> 25% of each run, Pallas kernels for 0% -> 0%
where the time goes in v1:
time: 1460 us; the launch traced here: 1440 us
  waiting for transfers between devices  961 us (66%)
  local copies, waits for them, and re-layouts  173 us (12%)
  matrix products  153 us (10%)
  other arithmetic  64.8 us (4%)
  blocking collectives  62.7 us (4%)
  between operations  18.1 us (1%)
    reduce_scatter x1, waiting for transfers between devices, scatter_every(): lax.psum_scatter(terms[0], 'dp', scatter_dimension=0, tiled=True)  325 us
    reduce_scatter x1, waiting for transfers between devices, scatter_every(): lax.psum_scatter(terms[3], 'dp', scatter_dimension=0, tiled=True)  124 us
    reduce_scatter x1, waiting for transfers between devices, scatter_every(): lax.psum_scatter(terms[4], 'dp', scatter_dimension=1, tiled=True)  124 us
    all_gather x1, waiting for transfers between devices, gather_weights(): lax.all_gather(modulation_weight, 'dp', axis=0, tiled=True)  112 us
    psum x1, blocking collectives, body(): lax.psum((bias_sums[0], bias_sums[1], bias_sums[2], bias_sums[3], bias_su...  62.7 us
    ppermute x8, waiting for transfers between devices, doubled_up(): theirs = lax.ppermute(grown, axis, [(d, d ^ reach) for d in range(ways)])  58.1 us
    scatter x2, local copies, waits for them, and re-layouts, run_micro(): block_mb = tokens_mb.at[batch_rows, order_mb].set(routed_out.astype(bf16))  53.3 us
    scatter x2, local copies, waits for them, and re-layouts, run_micro(): grad_mb.at[batch_rows, order_mb].set(grad_total.astype(bf16))  53.1 us
  transfers between devices with their start and end apart: 26, of which 19 were waited for; matrix products, arithmetic and copies ran while one was open for 25% of the time, Pallas kernels for 0%

profile of v1, /device:TPU:0, one launch (start us, length us, event | category | flops | bytes accessed | tf_op | source)
XLA Modules:
  0.0 1441.0 jit_solution(16123866024744263452)
XLA Ops:
  13.5 3.0 gather_fusion
  17.9 3.0 gather_fusion.1
  22.3 112.2 %all-gather.6.cloned.1.call-done = bf16[1152,6912]{1,0:T(8,128)(2,1)} async-done(((bf16[72,6912]{1,0:T(8,128)(2,1)}), bf16[1152,6912]{1,0:T(8,128)(2,1)}) %all-gather.6.cloned.1.call-update) | async-done | bytes 15925264 | tf_op jit(solution)/shard_map/all_gather | solution.py:44
  134.5 7.7 convolution_add_fusion.1
  142.9 43.7 %all-gather.8.cloned.1.call-done = bf16[3,1152,576]{2,1,0:T(8,128)(2,1)} async-done(((bf16[3,72,576]{2,1,0:T(8,128)(2,1)}), bf16[3,1152,576]{2,1,0:T(8,128)(2,1)}) %all-gather.8.cloned.1.call-update) | async-done | bytes 3981328 | tf_op jit(solution)/shard_map/all_gather | solution.py:45
  186.6 4.7 fusion.67
  193.8 32.9 %all-gather.10.cloned.1.call-done = bf16[576,1152]{0,1:T(8,128)(2,1)} async-done(((bf16[576,72]{0,1:T(8,128)(2,1)}), bf16[576,1152]{0,1:T(8,128)(2,1)}) %all-gather.10.cloned.1.call-update) | async-done | bytes 1327120 | tf_op jit(solution)/shard_map/all_gather | solution.py:46
  226.7 3.0 fusion.76
  229.8 8.1 convolution_add_fusion.2
  238.1 4.7 fusion.64
  251.6 28.2 %reduce-scatter.15.cloned.1.call-done = f32[2,128,576]{1,2,0:T(8,128)} async-done(((f32[2,128,1152]{1,2,0:T(8,128)}), f32[2,128,576]{1,2,0:T(8,128)}) %reduce-scatter.15.cloned.1.call-update) | async-done | bytes 589840 | tf_op jit(solution)/shard_map/reduce_scatter | solution.py:38
  283.0 3.8 gather_fusion.2
  290.3 5.1 collective-permute-done
  295.4 4.9 fusion.189
  300.6 37.3 %all-gather.12.cloned.1.call-done = bf16[1152,2304]{1,0:T(8,128)(2,1)} async-done(((bf16[72,2304]{1,0:T(8,128)(2,1)}), bf16[1152,2304]{1,0:T(8,128)(2,1)}) %all-gather.12.cloned.1.call-update) | async-done | bytes 5308432 | tf_op jit(solution)/shard_map/all_gather | solution.py:47
  338.0 5.9 fusion.27
  343.9 51.2 %all-gather.14.cloned.1.call-done = bf16[2304,1152]{0,1:T(8,128)(2,1)} async-done(((bf16[2304,72]{0,1:T(8,128)(2,1)}), bf16[2304,1152]{0,1:T(8,128)(2,1)}) %all-gather.14.cloned.1.call-update) | async-done | bytes 5308432 | tf_op jit(solution)/shard_map/all_gather | solution.py:48
  395.1 7.0 fusion.202
  403.2 2.6 fusion.13
  406.4 3.8 gather_fusion.3
  414.9 4.6 fusion.30
  419.6 4.1 fusion.203
  424.7 2.6 fusion.11
  427.4 5.9 fusion.9
  437.6 5.9 fusion.7
  443.8 17.0 %reduce-scatter.27.cloned.1.call-done = f32[2,128,576]{1,2,0:T(8,128)} async-done(((f32[2,128,1152]{1,2,0:T(8,128)}), f32[2,128,576]{1,2,0:T(8,128)}) %reduce-scatter.27.cloned.1.call-update) | async-done | bytes 589840 | tf_op jit(solution)/shard_map/reduce_scatter | solution.py:38
  464.8 3.0 multiply_reduce_fusion.2
  467.9 11.6 collective-permute-done.6
  480.1 4.2 multiply_reduce_fusion.9
  492.5 4.6 fusion.37
  498.2 4.8 multiply_reduce_fusion.8
  509.2 4.6 fusion.34
  515.0 3.1 fusion.140
  518.2 4.4 fusion.2
  522.7 13.8 copy.156
  536.6 2.2 convolution_bitcast_fusion.5
  538.9 2.6 fusion.33
  541.8 3.8 convolution_bitcast_fusion.1
  545.7 5.5 fusion
  551.3 3.4 convolution_bitcast_fusion.3
  554.8 5.2 fusion.1
  564.1 14.6 %collective-permute-done.1 = f32[2,128,576]{1,2,0:T(8,128)} collective-permute-done((f32[2,128,576]{1,2,0:T(8,128)}, f32[2,128,576]{1,2,0:T(8,128)}, u32[]{:S(2)}, u32[]{:S(2)}) %collective-permute-start.1) | collective-permute-done | bytes 589856 | tf_op jit(solution)/shard_map/ppermute | solution.py:15
  578.7 4.1 fusion.80
  582.9 8.4 collective-permute-done.3
  591.3 4.1 fusion.82
  595.4 8.6 collective-permute-done.5
  606.0 8.5 collective-permute-done.7
  615.4 2.6 fusion.96
  620.1 12.8 fusion.182
  632.9 24.0 %convolution_add_fusion = f32[1152,6912]{1,0:T(8,128)} fusion(f32[1152,6912]{1,0:T(8,128)} %fusion.182, bf16[2,6912]{1,0:T(2,128)(2,1)S(1)} %bitcast.367, bf16[4,1152]{1,0:T(4,128)(2,1)S(1)} %copy-done.80), kind=kOutput, calls=%fused_computation.8 | convolution fusion | flops 39826944 | bytes 63733248 | tf_op jit(solution)/shard_map/bd,be->de/dot_general | solution.py:315
  661.6 26.6 %scatter_fusion = bf16[2,256,1152]{2,1,0:T(8,128)(2,1)S(1)} fusion(bf16[2,256,1152]{2,1,0:T(8,128)(2,1)S(1)} %copy-done.3, s32[256]{0:T(256)S(1)} %copy-done.11, bf16[256,1152]{1,0:T(8,128)(2,1)} %bitcast.324), kind=kCustom, calls=%fused_computation.4 | custom fusion | bytes 1771520 | tf_op jit(solution)/shard_map/scatter | solution.py:144
  688.8 26.7 %scatter_fusion.1 = bf16[2,256,1152]{2,1,0:T(8,128)(2,1)S(1)} fusion(bf16[2,256,1152]{2,1,0:T(8,128)(2,1)S(1)} %copy-done.1, s32[256]{0:T(256)S(1)} %copy-done.10, bf16[256,1152]{1,0:T(8,128)(2,1)} %bitcast.323), kind=kCustom, calls=%fused_computation.5 | custom fusion | bytes 1771520 | tf_op jit(solution)/shard_map/scatter | solution.py:144
  721.0 2.6 fusion.101
  723.6 2.2 copy.143
  725.9 26.6 %scatter_fusion.2 = bf16[2,256,1152]{2,1,0:T(8,128)(2,1)S(1)} fusion(bf16[2,256,1152]{2,1,0:T(8,128)(2,1)S(1)} %copy-done.7, s32[256]{0:T(256)S(1)} %copy-done.11, bf16[256,1152]{1,0:T(8,128)(2,1)} %bitcast.325), kind=kCustom, calls=%fused_computation.6 | custom fusion | bytes 1771520 | tf_op jit(solution)/shard_map/scatter | solution.py:241
  753.5 3.7 fusion.104
  757.2 2.2 copy.153
  759.4 26.6 %scatter_fusion.3 = bf16[2,256,1152]{2,1,0:T(8,128)(2,1)S(1)} fusion(bf16[2,256,1152]{2,1,0:T(8,128)(2,1)S(1)} %copy-done.5, s32[256]{0:T(256)S(1)} %copy-done.10, bf16[256,1152]{1,0:T(8,128)(2,1)} %bitcast.326), kind=kCustom, calls=%fused_computation.7 | custom fusion | bytes 1771520 | tf_op jit(solution)/shard_map/scatter | solution.py:241
  788.8 62.7 %all-reduce.2 = (f32[6912]{0:T(1024)}, f32[2,576]{1,0:T(2,128)}, f32[1152]{0:T(1024)}, f32[2304]{0:T(1024)}, f32[1152]{0:T(1024)}) all-reduce(f32[6912]{0:T(1024)} %add.447, f32[2,576]{1,0:T(2,128)} %add.449, f32[1152]{0:T(1024)} %add.451, f32[2304]{0:T(1024)S(1)} %copy-done.124, f32[1152]{0:T(1024)} %add.455), channel_id=1, replica_groups=mesh['dp'=16,'mp'=2] {'dp'}, use_global_device_ids=true, to_apply=%region_50.52 | all-reduce | flops 12672 | bytes 101376 | tf_op jit(solution)/shard_map/psum | solution.py:326
  851.4 3.5 pad_maximum_fusion
  857.1 3.6 reduce-scatter.37.cloned.1.call-done
  860.6 123.8 %reduce-scatter.35.cloned.1.call-done = f32[2304,72]{0,1:T(8,128)} async-done(((f32[2304,1152]{0,1:T(8,128)}), f32[2304,72]{0,1:T(8,128)}) %reduce-scatter.35.cloned.1.call-update) | async-done | bytes 663568 | tf_op jit(solution)/shard_map/reduce_scatter | solution.py:58
  984.4 124.5 %reduce-scatter.33.cloned.1.call-done = f32[72,2304]{1,0:T(8,128)} async-done(((f32[1152,2304]{1,0:T(8,128)}), f32[72,2304]{1,0:T(8,128)}) %reduce-scatter.33.cloned.1.call-update) | async-done | bytes 663568 | tf_op jit(solution)/shard_map/reduce_scatter | solution.py:57
  1108.9 325.1 %reduce-scatter.31.cloned.1.call-done = f32[72,6912]{1,0:T(8,128)} async-done(((f32[1152,6912]{1,0:T(8,128)}), f32[72,6912]{1,0:T(8,128)}) %reduce-scatter.31.cloned.1.call-update) | async-done | bytes 1990672 | tf_op jit(solution)/shard_map/reduce_scatter | solution.py:54
  (555 shorter events, 84.8 us)
Async XLA Ops:
  7.2 127.3 %all-gather.6.cloned.1.call-start = ((), (), s32[]{:S(2)}) async-start(), calls=%async_computation.12 | async-start | bytes 16920576 | tf_op jit(solution)/shard_map/all_gather | solution.py:44
  8.0 178.7 %all-gather.8.cloned.1.call-start = ((), (), s32[]{:S(2)}) async-start(), calls=%async_computation.13 | async-start | bytes 4700160 | tf_op jit(solution)/shard_map/all_gather | solution.py:45
  8.7 218.0 %all-gather.10.cloned.1.call-start = ((), (), s32[]{:S(2)}) async-start(), calls=%async_computation.14 | async-start | bytes 1566720 | tf_op jit(solution)/shard_map/all_gather | solution.py:46
  9.4 241.0 %reduce-scatter.19.cloned.1.call-start = ((), (), s32[]{:S(2)}) async-start(), calls=%async_computation.19 | async-start | bytes 1769472 | tf_op jit(solution)/shard_map/reduce_scatter | solution.py:38
  9.5 177.1 %copy-start.111 = (pred[2,128]{1,0:T(4,128)(4,1)}, pred[2,128]{1,0:T(4,128)(4,1)S(1)}, u32[]{:S(2)}) copy-start(pred[2,128]{1,0:T(4,128)(4,1)S(1)} %get-tuple-element.125) | copy-start | bytes 772
  9.5 228.5 %copy-start.103 = (pred[2,128]{1,0:T(4,128)(4,1)}, pred[2,128]{1,0:T(4,128)(4,1)S(1)}, u32[]{:S(2)}) copy-start(pred[2,128]{1,0:T(4,128)(4,1)S(1)} %get-tuple-element.124) | copy-start | bytes 772
  10.9 232.1 %copy-start.155 = (pred[2,128]{1,0:T(4,128)(4,1)}, pred[2,128]{1,0:T(4,128)(4,1)S(1)}, u32[]{:S(2)}) copy-start(pred[2,128]{1,0:T(4,128)(4,1)S(1)} %iota_compare_fusion.2) | copy-start | bytes 772
  11.6 232.7 %copy-start.133 = (f32[8,72]{1,0:T(8,128)}, f32[8,72]{1,0:T(8,128)S(1)}, u32[]{:S(2)}) copy-start(f32[8,72]{1,0:T(8,128)S(1)} %add.391) | copy-start | bytes 6916
  11.7 231.3 %copy-start.99 = (f32[8,72]{1,0:T(8,128)}, f32[8,72]{1,0:T(8,128)S(1)}, u32[]{:S(2)}) copy-start(f32[8,72]{1,0:T(8,128)S(1)} %add.394) | copy-start | bytes 6916
  16.9 221.1 %copy-start.14 = (bf16[2,128,1152]{1,2,0:T(8,128)(2,1)}, bf16[2,128,1152]{1,2,0:T(8,128)(2,1)S(1)}, u32[]{:S(2)}) copy-start(bf16[2,128,1152]{1,2,0:T(8,128)(2,1)S(1)} %copy.124) | copy-start | bytes 1769476
  17.1 220.9 %copy-start.130 = (f32[2,128]{1,0:T(2,128)}, f32[2,128]{1,0:T(2,128)S(1)}, u32[]{:S(2)}) copy-start(f32[2,128]{1,0:T(2,128)S(1)} %broadcast_multiply_fusion.3) | copy-start | bytes 3076
  21.0 113.5 %copy-start.79 = (bf16[4,1152]{1,0:T(4,128)(2,1)S(1)}, bf16[4,1152]{1,0:T(4,128)(2,1)}, u32[]{:S(2)}) copy-start(bf16[4,1152]{1,0:T(4,128)(2,1)} %param.19) | copy-start | bytes 27652
  21.3 165.3 %copy-start.12 = (bf16[2,128,1152]{1,2,0:T(8,128)(2,1)}, bf16[2,128,1152]{1,2,0:T(8,128)(2,1)S(1)}, u32[]{:S(2)}) copy-start(bf16[2,128,1152]{1,2,0:T(8,128)(2,1)S(1)} %copy.129) | copy-start | bytes 1769476
  21.5 165.1 %copy-start.126 = (f32[2,128]{1,0:T(2,128)}, f32[2,128]{1,0:T(2,128)S(1)}, u32[]{:S(2)}) copy-start(f32[2,128]{1,0:T(2,128)S(1)} %broadcast_multiply_fusion.1) | copy-start | bytes 3076
  22.3 164.4 %copy-start.162 = (f32[2,128]{1,0:T(2,128)}, f32[2,128]{1,0:T(2,128)S(1)}, u32[]{:S(2)}) copy-start(f32[2,128]{1,0:T(2,128)S(1)} %fusion.170) | copy-start | bytes 3076
  142.9 48.5 %copy-start.136 = (f32[2,1,1,1152]{3,0,1,2:T(2,128)}, f32[2,1,1,1152]{3,0,1,2:T(2,128)S(1)}, u32[]{:S(2)}) copy-start(f32[2,1,1,1152]{3,0,1,2:T(2,128)S(1)} %copy.213) | copy-start | bytes 27652
  142.9 48.4 %copy-start.83 = (f32[2,1,1,1152]{3,0,1,2:T(2,128)}, f32[2,1,1,1152]{3,0,1,2:T(2,128)S(1)}, u32[]{:S(2)}) copy-start(f32[2,1,1,1152]{3,0,1,2:T(2,128)S(1)} %copy.214) | copy-start | bytes 27652
  193.8 35.9 %copy-start.72 = (bf16[2,8,72,128]{3,2,1,0:T(8,128)(2,1)}, bf16[2,8,72,128]{3,2,1,0:T(8,128)(2,1)S(1)}, u32[]{:S(2)}) copy-start(bf16[2,8,72,128]{3,2,1,0:T(8,128)(2,1)S(1)} %convolution_convert_fusion) | copy-start | bytes 884740
  229.7 50.1 %reduce-scatter.15.cloned.1.call-start = ((), (), s32[]{:S(2)}) async-start(), calls=%async_computation.15 | async-start | bytes 1769472 | tf_op jit(solution)/shard_map/reduce_scatter | solution.py:38
  247.5 90.4 %all-gather.12.cloned.1.call-start = ((), (), s32[]{:S(2)}) async-start(), calls=%async_computation.16 | async-start | bytes 5640192 | tf_op jit(solution)/shard_map/all_gather | solution.py:47
  248.1 147.0 %all-gather.14.cloned.1.call-start = ((), (), s32[]{:S(2)}) async-start(), calls=%async_computation.17 | async-start | bytes 5640192 | tf_op jit(solution)/shard_map/all_gather | solution.py:48
  248.9 187.2 %reduce-scatter.23.cloned.1.call-start = ((), (), s32[]{:S(2)}) async-start(), calls=%async_computation.21 | async-start | bytes 1769472 | tf_op jit(solution)/shard_map/reduce_scatter | solution.py:38
  250.4 39.8 %collective-permute-start.2 = (f32[2,128,576]{1,2,0:T(8,128)}, f32[2,128,576]{1,2,0:T(8,128)S(1)}, u32[]{:S(2)}, u32[]{:S(2)}) collective-permute-start(f32[2,128,576]{1,2,0:T(8,128)} %reduce-scatter.19.cloned.1.call-done), channel_id=1, source_target_pairs={{0,1},{1,0},{2,3},{3,2},{4,5},{5,4},{6,7},{7,6},{8,9},{9,8},{10,11... | collective-permute-start | bytes 1769480 | tf_op jit(solution)/shard_map/ppermute | solution.py:15
  279.8 15.6 %collective-permute-start = (f32[2,128,576]{1,2,0:T(8,128)}, f32[2,128,576]{1,2,0:T(8,128)}, u32[]{:S(2)}, u32[]{:S(2)}) collective-permute-start(f32[2,128,576]{1,2,0:T(8,128)} %reduce-scatter.15.cloned.1.call-done), channel_id=1, source_target_pairs={{0,1},{1,0},{2,3},{3,2},{4,5},{5,4},{6,7},{7,6},{8,9},{9,8},{10,11... | collective-permute-start | bytes 1769480 | tf_op jit(solution)/shard_map/ppermute | solution.py:15
  283.0 123.3 %copy-start.4 = (bf16[2,256,1152]{2,1,0:T(8,128)(2,1)}, bf16[2,256,1152]{2,1,0:T(8,128)(2,1)S(1)}, u32[]{:S(2)}) copy-start(bf16[2,256,1152]{2,1,0:T(8,128)(2,1)S(1)} %get-tuple-element.97) | copy-start | bytes 3538948
  300.4 37.6 %copy-start.94 = (f32[2304]{0:T(1024)S(1)}, f32[2304]{0:T(1024)}, u32[]{:S(2)}) copy-start(f32[2304]{0:T(1024)} %convert_element_type.181) | copy-start | bytes 27652
  300.4 37.6 %copy-start.96 = (f32[2,1,1,1152]{3,0,1,2:T(2,128)S(1)}, f32[2,1,1,1152]{3,0,1,2:T(2,128)}, u32[]{:S(2)}) copy-start(f32[2,1,1,1152]{3,0,1,2:T(2,128)} %copy.216) | copy-start | bytes 27652
  300.4 43.5 %copy-start.109 = (f32[2,128]{1,0:T(2,128)}, f32[2,128]{1,0:T(2,128)S(1)}, u32[]{:S(2)}) copy-start(f32[2,128]{1,0:T(2,128)S(1)} %broadcast_multiply_fusion.2) | copy-start | bytes 3076
  300.6 37.4 %copy-start.178 = (f32[2,128]{1,0:T(2,128)}, f32[2,128]{1,0:T(2,128)S(1)}, u32[]{:S(2)}) copy-start(f32[2,128]{1,0:T(2,128)S(1)} %multiply_reduce_fusion.7) | copy-start | bytes 3076
  300.6 43.3 %copy-start.122 = (f32[2,128]{1,0:T(2,128)}, f32[2,128]{1,0:T(2,128)S(1)}, u32[]{:S(2)}) copy-start(f32[2,128]{1,0:T(2,128)S(1)} %fusion.169) | copy-start | bytes 3076
  338.0 57.1 %copy-start.30 = (bf16[2,128,1152]{1,2,0:T(8,128)(2,1)S(1)}, bf16[2,128,1152]{1,2,0:T(8,128)(2,1)}, u32[]{:S(2)}) copy-start(bf16[2,128,1152]{1,2,0:T(8,128)(2,1)} %copy.134) | copy-start | bytes 1769476
  338.0 57.1 %copy-start.104 = (pred[2,128]{1,0:T(4,128)(4,1)S(1)}, pred[2,128]{1,0:T(4,128)(4,1)}, u32[]{:S(2)}) copy-start(pred[2,128]{1,0:T(4,128)(4,1)} %copy-done.103) | copy-start | bytes 772
  338.0 57.1 %copy-start.107 = (f32[2,1,1,1152]{3,0,1,2:T(2,128)S(1)}, f32[2,1,1,1152]{3,0,1,2:T(2,128)}, u32[]{:S(2)}) copy-start(f32[2,1,1,1152]{3,0,1,2:T(2,128)} %copy.218) | copy-start | bytes 27652
  338.0 57.1 %copy-start.156 = (pred[2,128]{1,0:T(4,128)(4,1)S(1)}, pred[2,128]{1,0:T(4,128)(4,1)}, u32[]{:S(2)}) copy-start(pred[2,128]{1,0:T(4,128)(4,1)} %copy-done.155) | copy-start | bytes 772
  405.9 54.9 %reduce-scatter.27.cloned.1.call-start = ((), (), s32[]{:S(2)}) async-start(), calls=%async_computation.23 | async-start | bytes 1769472 | tf_op jit(solution)/shard_map/reduce_scatter | solution.py:38
  411.7 85.7 %copy-start.28 = (bf16[2,128,1152]{1,2,0:T(8,128)(2,1)}, bf16[2,128,1152]{1,2,0:T(8,128)(2,1)S(1)}, u32[]{:S(2)}) copy-start(bf16[2,128,1152]{1,2,0:T(8,128)(2,1)S(1)} %copy.144) | copy-start | bytes 1769476
  427.3 133.2 %reduce-scatter.17.cloned.1.call-start = ((), (), s32[]{:S(2)}) async-start(), calls=%async_computation.18 | async-start | bytes 1769472 | tf_op jit(solution)/shard_map/reduce_scatter | solution.py:38
  433.3 127.3 %reduce-scatter.21.cloned.1.call-start = ((), (), s32[]{:S(2)}) async-start(), calls=%async_computation.20 | async-start | bytes 1769472 | tf_op jit(solution)/shard_map/reduce_scatter | solution.py:38
  436.0 26.1 %collective-permute-start.4 = (f32[2,128,576]{1,2,0:T(8,128)}, f32[2,128,576]{1,2,0:T(8,128)}, u32[]{:S(2)}, u32[]{:S(2)}) collective-permute-start(f32[2,128,576]{1,2,0:T(8,128)} %reduce-scatter.23.cloned.1.call-done), channel_id=1, source_target_pairs={{0,1},{1,0},{2,3},{3,2},{4,5},{5,4},{6,7},{7,6},{8,9},{9,8},{10,11... | collective-permute-start | bytes 1769480 | tf_op jit(solution)/shard_map/ppermute | solution.py:15
  443.5 120.4 %reduce-scatter.25.cloned.1.call-start = ((), (), s32[]{:S(2)}) async-start(), calls=%async_computation.22 | async-start | bytes 1769472 | tf_op jit(solution)/shard_map/reduce_scatter | solution.py:38
  460.7 18.7 %collective-permute-start.6 = (f32[2,128,576]{1,2,0:T(8,128)}, f32[2,128,576]{1,2,0:T(8,128)S(1)}, u32[]{:S(2)}, u32[]{:S(2)}) collective-permute-start(f32[2,128,576]{1,2,0:T(8,128)} %reduce-scatter.27.cloned.1.call-done), channel_id=1, source_target_pairs={{0,1},{1,0},{2,3},{3,2},{4,5},{5,4},{6,7},{7,6},{8,9},{9,8},{10,11... | collective-permute-start | bytes 1769480 | tf_op jit(solution)/shard_map/ppermute | solution.py:15
  497.1 85.7 %reduce-scatter.29.cloned.1.call-start = ((), (), s32[]{:S(2)}) async-start(), calls=%async_computation.24 | async-start | bytes 1769472 | tf_op jit(solution)/shard_map/reduce_scatter | solution.py:38
  513.9 341.1 %all-reduce.5.cloned.1.call-start = ((), (), s32[]{:S(2)}) async-start(), calls=%async_computation.28 | async-start | bytes 23592960
  536.5 324.1 %reduce-scatter.37.cloned.1.call-start = ((), (), s32[]{:S(2)}) async-start(), calls=%async_computation.29 | async-start | bytes 3133440
  541.5 443.0 %reduce-scatter.35.cloned.1.call-start = ((), (), s32[]{:S(2)}) async-start(), calls=%async_computation.27 | async-start | bytes 11280384 | tf_op jit(solution)/shard_map/reduce_scatter | solution.py:58
  551.2 557.7 %reduce-scatter.33.cloned.1.call-start = ((), (), s32[]{:S(2)}) async-start(), calls=%async_computation.26 | async-start | bytes 11280384 | tf_op jit(solution)/shard_map/reduce_scatter | solution.py:57
  560.0 873.9 %reduce-scatter.31.cloned.1.call-start = ((), (), s32[]{:S(2)}) async-start(), calls=%async_computation.25 | async-start | bytes 33841152 | tf_op jit(solution)/shard_map/reduce_scatter | solution.py:54
  560.6 18.1 %collective-permute-start.1 = (f32[2,128,576]{1,2,0:T(8,128)}, f32[2,128,576]{1,2,0:T(8,128)}, u32[]{:S(2)}, u32[]{:S(2)}) collective-permute-start(f32[2,128,576]{1,2,0:T(8,128)} %reduce-scatter.17.cloned.1.call-done), channel_id=1, source_target_pairs={{0,1},{1,0},{2,3},{3,2},{4,5},{5,4},{6,7},{7,6},{8,9},{9,8},{10,11... | collective-permute-start | bytes 1769480 | tf_op jit(solution)/shard_map/ppermute | solution.py:15
  560.7 30.6 %collective-permute-start.3 = (f32[2,128,576]{1,2,0:T(8,128)}, f32[2,128,576]{1,2,0:T(8,128)}, u32[]{:S(2)}, u32[]{:S(2)}) collective-permute-start(f32[2,128,576]{1,2,0:T(8,128)} %reduce-scatter.21.cloned.1.call-done), channel_id=1, source_target_pairs={{0,1},{1,0},{2,3},{3,2},{4,5},{5,4},{6,7},{7,6},{8,9},{9,8},{10,11... | collective-permute-start | bytes 1769480 | tf_op jit(solution)/shard_map/ppermute | solution.py:15
  564.0 40.0 %collective-permute-start.5 = (f32[2,128,576]{1,2,0:T(8,128)}, f32[2,128,576]{1,2,0:T(8,128)}, u32[]{:S(2)}, u32[]{:S(2)}) collective-permute-start(f32[2,128,576]{1,2,0:T(8,128)} %reduce-scatter.25.cloned.1.call-done), channel_id=1, source_target_pairs={{0,1},{1,0},{2,3},{3,2},{4,5},{5,4},{6,7},{7,6},{8,9},{9,8},{10,11... | collective-permute-start | bytes 1769480 | tf_op jit(solution)/shard_map/ppermute | solution.py:15
  582.8 21.1 %copy-start.38 = (f32[2,128,576]{1,2,0:T(8,128)S(1)}, f32[2,128,576]{1,2,0:T(8,128)}, u32[]{:S(2)}) copy-start(f32[2,128,576]{1,2,0:T(8,128)} %reduce-scatter.25.cloned.1.call-done) | copy-start | bytes 1769476
  582.8 21.1 %copy-start.82 = (f32[2,1,1,1152]{3,0,1,2:T(2,128)S(1)}, f32[2,1,1,1152]{3,0,1,2:T(2,128)}, u32[]{:S(2)}) copy-start(f32[2,1,1,1152]{3,0,1,2:T(2,128)} %copy-done.81) | copy-start | bytes 27652
  582.8 21.1 %copy-start.106 = (pred[2,128]{1,0:T(4,128)(4,1)S(1)}, pred[2,128]{1,0:T(4,128)(4,1)}, u32[]{:S(2)}) copy-start(pred[2,128]{1,0:T(4,128)(4,1)} %copy-done.103) | copy-start | bytes 772
  582.8 21.1 %copy-start.131 = (f32[2,128]{1,0:T(2,128)S(1)}, f32[2,128]{1,0:T(2,128)}, u32[]{:S(2)}) copy-start(f32[2,128]{1,0:T(2,128)} %copy-done.130) | copy-start | bytes 3076
  582.8 31.7 %collective-permute-start.7 = (f32[2,128,576]{1,2,0:T(8,128)}, f32[2,128,576]{1,2,0:T(8,128)S(1)}, u32[]{:S(2)}, u32[]{:S(2)}) collective-permute-start(f32[2,128,576]{1,2,0:T(8,128)} %reduce-scatter.29.cloned.1.call-done), channel_id=1, source_target_pairs={{0,1},{1,0},{2,3},{3,2},{4,5},{5,4},{6,7},{7,6},{8,9},{9,8},{10,11... | collective-permute-start | bytes 1769480 | tf_op jit(solution)/shard_map/ppermute | solution.py:15
  661.6 26.6 %copy-start.153 = (f32[1152]{0:T(1024)S(1)}, f32[1152]{0:T(1024)}, u32[]{:S(2)}) copy-start(f32[1152]{0:T(1024)} %get-tuple-element.81) | copy-start | bytes 13828
  661.6 26.6 %copy-start.154 = (f32[1152]{0:T(1024)S(1)}, f32[1152]{0:T(1024)}, u32[]{:S(2)}) copy-start(f32[1152]{0:T(1024)} %get-tuple-element.79) | copy-start | bytes 13828
  661.6 27.2 %copy-start.1 = (bf16[2,256,1152]{2,1,0:T(8,128)(2,1)S(1)}, bf16[2,256,1152]{2,1,0:T(8,128)(2,1)}, u32[]{:S(2)}) copy-start(bf16[2,256,1152]{2,1,0:T(8,128)(2,1)} %copy-done) | copy-start | bytes 3538948
  661.6 27.2 %copy-start.10 = (s32[256]{0:T(256)S(1)}, s32[256]{0:T(256)}, u32[]{:S(2)}) copy-start(s32[256]{0:T(256)} %get-tuple-element.128) | copy-start | bytes 3076
  688.8 26.8 %copy-start.149 = (f32[1152]{0:T(1024)S(1)}, f32[1152]{0:T(1024)}, u32[]{:S(2)}) copy-start(f32[1152]{0:T(1024)} %get-tuple-element.71) | copy-start | bytes 13828
  688.8 26.8 %copy-start.150 = (f32[1152]{0:T(1024)S(1)}, f32[1152]{0:T(1024)}, u32[]{:S(2)}) copy-start(f32[1152]{0:T(1024)} %get-tuple-element.69) | copy-start | bytes 13828
  725.9 27.6 %copy-start.116 = (pred[2,128]{1,0:T(4,128)(4,1)S(1)}, pred[2,128]{1,0:T(4,128)(4,1)}, u32[]{:S(2)}) copy-start(pred[2,128]{1,0:T(4,128)(4,1)} %copy-done.111) | copy-start | bytes 772
  725.9 27.6 %copy-start.129 = (f32[2,128]{1,0:T(2,128)S(1)}, f32[2,128]{1,0:T(2,128)}, u32[]{:S(2)}) copy-start(f32[2,128]{1,0:T(2,128)} %copy-done.126) | copy-start | bytes 3076
  759.4 29.4 %copy-start.124 = (f32[2304]{0:T(1024)S(1)}, f32[2304]{0:T(1024)}, u32[]{:S(2)}) copy-start(f32[2304]{0:T(1024)} %add.453) | copy-start | bytes 27652
  (154 other events, 646.5 us)
Sparse Core Ops, SparseCore 0:
  10.2 124.2 all-gather.5
  136.7 49.9 all-gather.7
  188.8 37.8 all-gather.9
  229.8 20.5 reduce-scatter.18
  253.2 26.5 reduce-scatter.14
  281.9 56.0 all-gather.11
  340.1 54.9 all-gather.13
  406.0 20.3 reduce-scatter.22
  428.7 31.9 reduce-scatter.26
  462.8 26.5 reduce-scatter.16
  492.3 24.7 reduce-scatter.20
  519.2 21.7 reduce-scatter.24
  543.3 25.4 reduce-scatter.28
  572.4 218.3 all-reduce.4
  795.1 65.4 reduce-scatter.36
  865.1 119.2 reduce-scatter.34
  988.9 119.9 reduce-scatter.32
  1113.6 320.3 reduce-scatter.30
